TPU v7x, 32 devices: a whole 2x2x4 slice. The times are simulated.
32 devices in a mesh: dp: 8 (over z, x), tensor: 4 (over y, core).
Axes of the slice: x: 2, y: 2, z: 4, core: 2. Of those that a mesh axis runs over, the one named last changes fastest.
Arguments:
- layer_input: bfloat16 [32768, 1024], P(('dp', 'tensor')), may hold values from -6 to 6
- row_ids: int32 [32768], P('dp'), may hold values from 0 to 1, as said below
- input_gain: bfloat16 [1024], replicated, may hold values from 0.5 to 1.5
- input_shift: bfloat16 [1024], replicated, may hold values from -1.796875 to 1.796875
- query_weight: bfloat16 [1024, 1024], P(None, 'tensor'), may hold values from -0.1875 to 0.1875
- query_bias: bfloat16 [1024], P('tensor'), may hold values from -1.796875 to 1.796875
- key_weight: bfloat16 [1024, 1024], P(None, 'tensor'), may hold values from -0.1875 to 0.1875
- value_weight: bfloat16 [1024, 1024], P(None, 'tensor'), may hold values from -0.1875 to 0.1875
- value_bias: bfloat16 [1024], P('tensor'), may hold values from -1.796875 to 1.796875
- dense_weight: bfloat16 [1024, 1024], P('tensor'), may hold values from -0.75 to 0.75
- dense_bias: bfloat16 [1024], replicated, may hold values from -1.796875 to 1.796875
- post_gain: bfloat16 [1024], replicated, may hold values from 0.5 to 1.5
- post_shift: bfloat16 [1024], replicated, may hold values from -1.796875 to 1.796875
- up_weight: bfloat16 [1024, 4096], P(None, 'tensor'), may hold values from -0.1875 to 0.1875
- up_bias: bfloat16 [4096], P('tensor'), may hold values from -1.796875 to 1.796875
- down_weight: bfloat16 [4096, 1024], P('tensor'), may hold values from -0.1875 to 0.1875
- down_bias: bfloat16 [1024], replicated, may hold values from -1.796875 to 1.796875
- cotangent: bfloat16 [32768, 1024], P(('dp', 'tensor')), may hold values from -6 to 6
Outputs:
- layer_output: bfloat16 [32768, 1024], P(('dp', 'tensor'))
- input_grad: float32 [32768, 1024], P(('dp', 'tensor'))
- input_gain_grad: float32 [1024], replicated
- input_shift_grad: float32 [1024], replicated
- query_weight_grad: float32 [1024, 1024], P(None, 'tensor')
- query_bias_grad: float32 [1024], P('tensor')
- key_weight_grad: float32 [1024, 1024], P(None, 'tensor')
- value_weight_grad: float32 [1024, 1024], P(None, 'tensor')
- value_bias_grad: float32 [1024], P('tensor')
- dense_weight_grad: float32 [1024, 1024], P('tensor')
- dense_bias_grad: float32 [1024], replicated
- post_gain_grad: float32 [1024], replicated
- post_shift_grad: float32 [1024], replicated
- up_weight_grad: float32 [1024, 4096], P(None, 'tensor')
- up_bias_grad: float32 [4096], P('tensor')
- down_weight_grad: float32 [4096, 1024], P('tensor')
- down_bias_grad: float32 [1024], replicated
Inputs may be any that keep to these rules, and one draw needn't show every extreme that they name: `row_ids`: within each data group of 4096 consecutive tokens, the tokens form rows of 2048 or 4096 consecutive tokens, each row starting at a multiple of its own length within the group; every token of a row carries the index, within its group, of the row's last block of 2048 tokens, so ids never fall within a group and two rows of a group never share an id.
All inputs are finite; a program needn't handle non-finite values.
Results may differ from a plain program's by a relative error of at most 0.013.
Values may be sent and summed in bfloat16 or wider, within the bound.
A program may use at most 576 MiB of HBM per device.

v0:
```python
import jax
import jax.numpy as jnp
from jax import lax
from jax.sharding import PartitionSpec as P

HEADS = 16
HD = 64
SHORT = 2048
BLOCK = 512
EPSILON = 1e-05


def layer_norm(inputs, gain_vec, shift_vec):
    center = jnp.mean(inputs, axis=-1, keepdims=True)
    centered = inputs - center
    spread = jnp.mean(centered * centered, axis=-1, keepdims=True)
    return centered * lax.rsqrt(spread + EPSILON) * gain_vec + shift_vec


def gelu_tanh(inputs):
    return jax.nn.gelu(inputs, approximate=True)


def split_heads(matrix, head_count):
    return matrix.reshape(matrix.shape[0], head_count, HD).transpose(1, 0, 2)


def join_heads(stacked):
    return stacked.transpose(1, 0, 2).reshape(stacked.shape[1], stacked.shape[0] * stacked.shape[2])


def block_scores(query_block, key_block, slopes, query_first, key_first, query_ids, key_ids):
    products = jnp.einsum(
        "hqd,hkd->hqk", query_block, key_block, preferred_element_type=jnp.float32
    )
    query_pos = query_first + jnp.arange(query_block.shape[1])
    key_pos = key_first + jnp.arange(key_block.shape[1])
    offsets = (key_pos[None, :] - query_pos[:, None]).astype(jnp.float32)
    scores = products * HD ** (-0.5) + slopes[:, None, None] * offsets[None]
    allowed = (query_ids[:, None] == key_ids[None, :]) & (offsets <= 0)
    return jnp.where(allowed[None], scores, -1e30)


def shards(
    layer_input,
    row_ids,
    input_gain,
    input_shift,
    query_weight,
    query_bias,
    key_weight,
    value_weight,
    value_bias,
    dense_weight,
    dense_bias,
    post_gain,
    post_shift,
    up_weight,
    up_bias,
    down_weight,
    down_bias,
    cotangent,
):
    group_len = row_ids.shape[0]
    head_cols = query_weight.shape[1]
    head_count = head_cols // HD
    window_len = 2 * SHORT
    block_count = group_len // BLOCK

    def block_bounds(block_index):
        row_first = block_index * BLOCK
        key_first = row_first // window_len * window_len
        return (row_first, key_first, row_first + BLOCK)

    inputs = layer_input.astype(jnp.float32)
    normed, norm_pull = jax.vjp(
        layer_norm, inputs, input_gain.astype(jnp.float32), input_shift.astype(jnp.float32)
    )
    normed_low = normed.astype(jnp.bfloat16)
    normed_all = lax.all_gather(normed_low, "tensor", axis=0, tiled=True)
    joined = jnp.concatenate([query_weight, key_weight, value_weight], axis=1)
    projected = jnp.dot(normed_all, joined, preferred_element_type=jnp.float32)
    queries = (projected[:, :head_cols] + query_bias.astype(jnp.float32)).astype(jnp.bfloat16)
    key_rows = projected[:, head_cols : 2 * head_cols].astype(jnp.bfloat16)
    values = (projected[:, 2 * head_cols :] + value_bias.astype(jnp.float32)).astype(jnp.bfloat16)
    query_heads = split_heads(queries, head_count)
    key_heads = split_heads(key_rows, head_count)
    value_heads = split_heads(values, head_count)
    head_index = lax.axis_index("tensor") * head_count + jnp.arange(head_count)
    slopes = jnp.exp2(-8.0 * (head_index + 1).astype(jnp.float32) / HEADS)
    out_blocks = []
    total_blocks = []
    for block_index in range(block_count):
        row_first, key_first, row_last = block_bounds(block_index)
        masked = block_scores(
            query_heads[:, row_first:row_last],
            key_heads[:, key_first:row_last],
            slopes,
            row_first,
            key_first,
            row_ids[row_first:row_last],
            row_ids[key_first:row_last],
        )
        log_total = jax.nn.logsumexp(masked, axis=-1, keepdims=True)
        prob_low = jnp.exp(masked - log_total).astype(jnp.bfloat16)
        out_blocks.append(
            jnp.einsum(
                "hqk,hkd->hqd",
                prob_low,
                value_heads[:, key_first:row_last],
                preferred_element_type=jnp.float32,
            )
        )
        total_blocks.append(log_total)
    mixed_heads = join_heads(jnp.concatenate(out_blocks, axis=1)).astype(jnp.bfloat16)
    attended = lax.psum_scatter(
        jnp.dot(mixed_heads, dense_weight, preferred_element_type=jnp.float32),
        "tensor",
        scatter_dimension=0,
        tiled=True,
    )
    residual = inputs + attended + dense_bias.astype(jnp.float32)
    post_rows, post_pull = jax.vjp(
        layer_norm, residual, post_gain.astype(jnp.float32), post_shift.astype(jnp.float32)
    )
    post_low = post_rows.astype(jnp.bfloat16)
    post_all = lax.all_gather(post_low, "tensor", axis=0, tiled=True)
    hidden = jnp.dot(post_all, up_weight, preferred_element_type=jnp.float32) + up_bias.astype(
        jnp.float32
    )
    active, gelu_pull = jax.vjp(gelu_tanh, hidden)
    active_low = active.astype(jnp.bfloat16)
    ffn_out = lax.psum_scatter(
        jnp.dot(active_low, down_weight, preferred_element_type=jnp.float32),
        "tensor",
        scatter_dimension=0,
        tiled=True,
    )
    layer_output = (residual + ffn_out + down_bias.astype(jnp.float32)).astype(jnp.bfloat16)
    grad_rows = cotangent.astype(jnp.float32)
    down_bias_part = jnp.sum(grad_rows, axis=0)
    grad_all = lax.all_gather(cotangent, "tensor", axis=0, tiled=True)
    act_grad = jnp.einsum("td,fd->tf", grad_all, down_weight, preferred_element_type=jnp.float32)
    hidden_grad = gelu_pull(act_grad)[0].astype(jnp.bfloat16)
    up_part = jnp.einsum("td,tf->df", post_all, hidden_grad, preferred_element_type=jnp.float32)
    down_part = jnp.einsum("tf,td->fd", active_low, grad_all, preferred_element_type=jnp.float32)
    up_bias_part = jnp.sum(hidden_grad.astype(jnp.float32), axis=0)
    post_grad = lax.psum_scatter(
        jnp.einsum("tf,df->td", hidden_grad, up_weight, preferred_element_type=jnp.float32),
        "tensor",
        scatter_dimension=0,
        tiled=True,
    )
    norm_grad_resid, post_gain_part, post_shift_part = post_pull(post_grad)
    resid_grad = grad_rows + norm_grad_resid
    dense_bias_part = jnp.sum(resid_grad, axis=0)
    attended_all = lax.all_gather(resid_grad.astype(jnp.bfloat16), "tensor", axis=0, tiled=True)
    dense_part = jnp.einsum(
        "tc,td->cd", mixed_heads, attended_all, preferred_element_type=jnp.float32
    )
    mixed_grad = jnp.einsum(
        "td,cd->tc", attended_all, dense_weight, preferred_element_type=jnp.float32
    ).astype(jnp.bfloat16)
    grad_heads = split_heads(mixed_grad, head_count)
    query_grads = []
    key_acc = jnp.zeros((head_count, group_len, HD), jnp.float32)
    value_acc = jnp.zeros((head_count, group_len, HD), jnp.float32)
    for block_index in range(block_count):
        row_first, key_first, row_last = block_bounds(block_index)
        query_block = query_heads[:, row_first:row_last]
        key_block = key_heads[:, key_first:row_last]
        value_block = value_heads[:, key_first:row_last]
        out_grad = grad_heads[:, row_first:row_last]
        masked = block_scores(
            query_block,
            key_block,
            slopes,
            row_first,
            key_first,
            row_ids[row_first:row_last],
            row_ids[key_first:row_last],
        )
        prob_full = jnp.exp(masked - total_blocks[block_index])
        prob_low = prob_full.astype(jnp.bfloat16)
        value_acc = value_acc.at[:, key_first:row_last].add(
            jnp.einsum("hqk,hqd->hkd", prob_low, out_grad, preferred_element_type=jnp.float32)
        )
        prob_grad = jnp.einsum(
            "hqd,hkd->hqk", out_grad, value_block, preferred_element_type=jnp.float32
        )
        row_dot = jnp.sum(prob_full * prob_grad, axis=-1, keepdims=True)
        score_grad = (prob_full * (prob_grad - row_dot)).astype(jnp.bfloat16)
        query_grads.append(
            jnp.einsum("hqk,hkd->hqd", score_grad, key_block, preferred_element_type=jnp.float32)
            * HD ** (-0.5)
        )
        key_acc = key_acc.at[:, key_first:row_last].add(
            jnp.einsum("hqk,hqd->hkd", score_grad, query_block, preferred_element_type=jnp.float32)
            * HD ** (-0.5)
        )
    query_grad = join_heads(jnp.concatenate(query_grads, axis=1)).astype(jnp.bfloat16)
    key_grad = join_heads(key_acc).astype(jnp.bfloat16)
    value_grad = join_heads(value_acc).astype(jnp.bfloat16)
    proj_grad = jnp.concatenate([query_grad, key_grad, value_grad], axis=1)
    joined_part = jnp.einsum("td,tc->dc", normed_all, proj_grad, preferred_element_type=jnp.float32)
    query_bias_part = jnp.sum(query_grad.astype(jnp.float32), axis=0)
    value_bias_part = jnp.sum(value_grad.astype(jnp.float32), axis=0)
    normed_grad = lax.psum_scatter(
        jnp.einsum("tc,dc->td", proj_grad, joined, preferred_element_type=jnp.float32),
        "tensor",
        scatter_dimension=0,
        tiled=True,
    )
    input_norm_grad, input_gain_part, input_shift_part = norm_pull(normed_grad)
    input_grad = resid_grad + input_norm_grad
    summed = lax.psum(
        (
            joined_part[:, :head_cols],
            query_bias_part,
            joined_part[:, head_cols : 2 * head_cols],
            joined_part[:, 2 * head_cols :],
            value_bias_part,
            dense_part,
            up_part,
            up_bias_part,
            down_part,
        ),
        "dp",
    )
    shared = lax.psum(
        (
            input_gain_part,
            input_shift_part,
            dense_bias_part,
            post_gain_part,
            post_shift_part,
            down_bias_part,
        ),
        ("dp", "tensor"),
    )
    return (
        layer_output,
        input_grad,
        shared[0],
        shared[1],
        summed[0],
        summed[1],
        summed[2],
        summed[3],
        summed[4],
        summed[5],
        shared[2],
        shared[3],
        shared[4],
        summed[6],
        summed[7],
        summed[8],
        shared[5],
    )


def solution(mesh):
    in_specs = (
        P(("dp", "tensor"), None),
        P("dp"),
        P(),
        P(),
        P(None, "tensor"),
        P("tensor"),
        P(None, "tensor"),
        P(None, "tensor"),
        P("tensor"),
        P("tensor", None),
        P(),
        P(),
        P(),
        P(None, "tensor"),
        P("tensor"),
        P("tensor", None),
        P(),
        P(("dp", "tensor"), None),
    )
    out_specs = (
        P(("dp", "tensor"), None),
        P(("dp", "tensor"), None),
        P(),
        P(),
        P(None, "tensor"),
        P("tensor"),
        P(None, "tensor"),
        P(None, "tensor"),
        P("tensor"),
        P("tensor", None),
        P(),
        P(),
        P(),
        P(None, "tensor"),
        P("tensor"),
        P("tensor", None),
        P(),
    )
    return jax.shard_map(shards, mesh=mesh, in_specs=in_specs, out_specs=out_specs, check_vma=False)
```

profile of v0, /device:TPU:0, one launch (start us, length us, event | category | flops | bytes accessed | tf_op | source)
XLA Modules:
  0.0 1910.5 jit_solution(7665269605376054188)
XLA Ops:
  60.0 17.7 all-gather.5.cloned.1.call-done
  204.8 18.3 fusion.230
  223.2 16.4 exponential_reduce_fusion
  319.2 125.6 %reduce-scatter.5.cloned.1.call-done = f32[1024,1024]{1,0:T(8,128)} async-done(((f32[4096,1024]{1,0:T(8,128)}), f32[1024,1024]{1,0:T(8,128)}) %reduce-scatter.5.cloned.1.call-update) | async-done | bytes 4194320 | tf_op jit(solution)/shard_map/reduce_scatter | solution.py:116
  453.0 57.8 %all-gather.7.cloned.1.call-done = bf16[4096,1024]{1,0:T(8,128)(2,1)} async-done(((bf16[1024,1024]{1,0:T(8,128)(2,1)}), bf16[4096,1024]{1,0:T(8,128)(2,1)}) %all-gather.7.cloned.1.call-update) | async-done | bytes 8388624 | tf_op jit(solution)/shard_map/all_gather | solution.py:127
  510.8 16.1 fusion.233
  526.9 43.8 %all-gather.9.cloned.1.call-done = bf16[4096,1024]{1,0:T(8,128)(2,1)} async-done(((bf16[1024,1024]{1,0:T(8,128)(2,1)}), bf16[4096,1024]{1,0:T(8,128)(2,1)}) %all-gather.9.cloned.1.call-update) | async-done | bytes 8388624 | tf_op jit(solution)/shard_map/all_gather | solution.py:142
  570.6 27.1 %convert_reduce_fusion = (f32[1024]{0:T(1024)}, bf16[4096,1024]{1,0:T(8,128)(2,1)S(1)}, bf16[4096,1024]{1,0:T(8,128)(2,1)}) fusion(f32[4096,1024]{1,0:T(8,128)} %fusion.233, f32[1024]{0:T(1024)S(1)} %convert_element_type.310, bf16[4096,1024]{1,0:T(8,128)(2,1)} %all-gather.9.cloned.1.call-done, bf16[1024,1024]{1,0:T(8,128)(2,1)S(1)} %copy-done), kind=kOutput, calls=%fused_computation.32 | convolution fusion | flops 8694791168 | bytes 44048384 | tf_op jit(solution)/shard_map/td,fd->tf/dot_general | solution.py:143
  613.3 16.6 fusion.234
  630.6 109.0 %reduce-scatter.9.cloned.1.call-done = f32[1024,1024]{1,0:T(8,128)} async-done(((f32[4096,1024]{1,0:T(8,128)}), f32[1024,1024]{1,0:T(8,128)}) %reduce-scatter.9.cloned.1.call-update) | async-done | bytes 4194320 | tf_op jit(solution)/shard_map/reduce_scatter | solution.py:148
  744.4 123.7 %reduce-scatter.7.cloned.1.call-done = f32[1024,1024]{1,0:T(8,128)} async-done(((f32[4096,1024]{1,0:T(8,128)}), f32[1024,1024]{1,0:T(8,128)}) %reduce-scatter.7.cloned.1.call-update) | async-done | bytes 4194320 | tf_op jit(solution)/shard_map/reduce_scatter | solution.py:133
  878.7 58.4 %all-gather.11.cloned.1.call-done = bf16[4096,1024]{1,0:T(8,128)(2,1)} async-done(((bf16[1024,1024]{1,0:T(8,128)(2,1)}), bf16[4096,1024]{1,0:T(8,128)(2,1)}) %all-gather.11.cloned.1.call-update) | async-done | bytes 8388624 | tf_op jit(solution)/shard_map/all_gather | solution.py:157
  993.5 16.4 multiply_reduce_fusion.2
  1009.9 21.0 %multiply_reduce_fusion.1 = (f32[4,512]{1,0:T(4,128)}, f32[4,512,3584]{2,1,0:T(8,128)}) fusion(f32[4,512,3584]{2,1,0:T(8,128)} %get-tuple-element.284, f32[4,512]{1,0:T(4,128)S(1)} %copy-done.39, bf16[4,4096,64]{1,2,0:T(8,128)(2,1)S(1)} %bitcast.87, bf16[4,4096,64]{1,2,0:T(8,128)(2,1)} %bitcast.116), kind=kOutput, calls=%fused_computation.6 | convolution fusion | flops 961542144 | bytes 60833792 | tf_op jit(solution)/shard_map/hqd,hkd->hqk/dot_general | solution.py:188
  1030.9 22.6 %multiply_reduce_fusion = (f32[4,512]{1,0:T(4,128)}, f32[4,512,4096]{2,1,0:T(8,128)}) fusion(f32[4,512,4096]{2,1,0:T(8,128)} %get-tuple-element.286, f32[4,512]{1,0:T(4,128)S(1)} %copy-done.43, bf16[4,4096,64]{1,2,0:T(8,128)(2,1)S(1)} %bitcast.88, bf16[4,4096,64]{1,2,0:T(8,128)(2,1)S(1)} %bitcast.117), kind=kOutput, calls=%fused_computation.1 | convolution fusion | flops 1098905600 | bytes 69484544 | tf_op jit(solution)/shard_map/hqd,hkd->hqk/dot_general | solution.py:188
  1119.1 16.5 convert_reduce_fusion.3
  1218.0 16.8 multiply_convert_fusion.2
  1254.7 24.6 %multiply_convert_fusion.1 = bf16[4,512,3584]{2,1,0:T(8,128)(2,1)} fusion(f32[4,512,3584]{2,1,0:T(8,128)} %get-tuple-element.300, f32[4,512,3584]{2,1,0:T(8,128)} %get-tuple-element.284, f32[4,512]{1,0:T(4,128)S(1)} %copy-done.84, f32[4,512]{1,0:T(4,128)S(1)} %copy-done.39), kind=kLoop, calls=%fused_computation.5 | loop fusion | flops 29360128 | bytes 73416704 | tf_op jit(solution)/shard_map/convert_element_type | solution.py:192
  1295.8 27.6 %multiply_convert_fusion = bf16[4,512,4096]{2,1,0:T(8,128)(2,1)} fusion(f32[4,512,4096]{2,1,0:T(8,128)} %get-tuple-element.302, f32[4,512,4096]{2,1,0:T(8,128)} %get-tuple-element.286, f32[4,512]{1,0:T(4,128)S(1)} %copy-done.83, f32[4,512]{1,0:T(4,128)S(1)} %copy-done.43), kind=kLoop, calls=%fused_computation | loop fusion | flops 33554432 | bytes 83902464 | tf_op jit(solution)/shard_map/convert_element_type | solution.py:192
  1370.4 18.2 fusion.237
  1407.5 22.4 %all-reduce.3 = (f32[256]{0:T(256)}, f32[256]{0:T(256)}, f32[1024]{0:T(1024)}) all-reduce(f32[256]{0:T(256)S(1)} %reduce_sum.360, f32[256]{0:T(256)S(1)} %reduce_sum.362, f32[1024]{0:T(1024)S(1)} %copy-done.92), channel_id=1, replica_groups=mesh['dp'=8,'tensor'=4] {'dp'}, use_global_device_ids=true, to_apply=%region_42.43 | all-reduce | flops 1536 | bytes 12288 | tf_op jit(solution)/shard_map/psum | solution.py:216
  1429.9 51.0 %reduce-scatter.11.cloned.1.call-done = f32[1024,1024]{1,0:T(8,128)} async-done(((f32[4096,1024]{1,0:T(8,128)}), f32[1024,1024]{1,0:T(8,128)}) %reduce-scatter.11.cloned.1.call-update) | async-done | bytes 4194320 | tf_op jit(solution)/shard_map/reduce_scatter | solution.py:208
  1490.8 44.6 %all-reduce.2 = (f32[1024]{0:T(1024)}, f32[1024]{0:T(1024)}, f32[1024]{0:T(1024)}, f32[1024]{0:T(1024)}, f32[1024]{0:T(1024)}, /*index=5*/f32[1024]{0:T(1024)}) all-reduce(f32[1024]{0:T(1024)S(1)} %get-tuple-element.227, f32[1024]{0:T(1024)S(1)} %get-tuple-element.230, ...), channel_id=1, replica_groups=mesh['dp'=8,'tensor'=4] {'dp','tensor'}, use_global_device_ids=true, to_apply=%region_37.38 | all-reduce | flops 6144 | bytes 49152 | tf_op jit(solution)/shard_map/psum | solution.py:230
  1535.4 355.9 %all-reduce.7.cloned.1.call-done = (f32[1024,256]{1,0:T(8,128)}, f32[1024,256]{1,0:T(8,128)}, f32[1024,256]{1,0:T(8,128)}, f32[256,1024]{1,0:T(8,128)}, f32[1024,1024]{1,0:T(8,128)}, /*index=5*/f32[1024,1024]{1,0:T(8,128)}) async-done(((f32[1024,256]{1,0:T(8,128)}, f32[1024,256]{1,0:T(8,128)}, f32[1024,256]{1,0:T(8,128)}, f32[256,1024]{1,0:T(8,128)}, f32[1024,1024]{1,0:T(8,128)}, ...) | async-done | bytes 12582928 | tf_op jit(solution)/shard_map/psum | solution.py:216
  (422 shorter events, 627.4 us)
Async XLA Ops:
  7.2 563.4 %copy-start = (bf16[1024,1024]{1,0:T(8,128)(2,1)S(1)}, bf16[1024,1024]{1,0:T(8,128)(2,1)}, u32[]{:S(2)}) copy-start(bf16[1024,1024]{1,0:T(8,128)(2,1)} %param.69) | copy-start | bytes 6291460
  7.2 70.5 %all-gather.5.cloned.1.call-start = ((), (), s32[]{:S(2)}) async-start(), calls=%async_computation.4 | async-start | bytes 10485760 | tf_op jit(solution)/shard_map/all_gather | solution.py:80
  16.6 428.2 %reduce-scatter.5.cloned.1.call-start = ((), (), s32[]{:S(2)}) async-start(), calls=%async_computation.5 | async-start | bytes 20971520 | tf_op jit(solution)/shard_map/reduce_scatter | solution.py:116
  94.4 145.1 %copy-start.66 = (f32[4,512]{1,0:T(4,128)}, f32[4,512]{1,0:T(4,128)S(1)}, u32[]{:S(2)}) copy-start(f32[4,512]{1,0:T(4,128)S(1)} %log_add_fusion.7) | copy-start | bytes 24580
  102.0 139.1 %copy-start.63 = (f32[4,512]{1,0:T(4,128)}, f32[4,512]{1,0:T(4,128)S(1)}, u32[]{:S(2)}) copy-start(f32[4,512]{1,0:T(4,128)S(1)} %log_add_fusion.6) | copy-start | bytes 24580
  110.2 133.3 %copy-start.59 = (f32[4,512]{1,0:T(4,128)}, f32[4,512]{1,0:T(4,128)S(1)}, u32[]{:S(2)}) copy-start(f32[4,512]{1,0:T(4,128)S(1)} %log_add_fusion.5) | copy-start | bytes 24580
  128.6 122.2 %copy-start.68 = (f32[4,512]{1,0:T(4,128)}, f32[4,512]{1,0:T(4,128)S(1)}, u32[]{:S(2)}) copy-start(f32[4,512]{1,0:T(4,128)S(1)} %log_add_fusion.4) | copy-start | bytes 24580
  151.3 109.0 %copy-start.51 = (f32[4,512]{1,0:T(4,128)}, f32[4,512]{1,0:T(4,128)S(1)}, u32[]{:S(2)}) copy-start(f32[4,512]{1,0:T(4,128)S(1)} %log_add_fusion.3) | copy-start | bytes 24580
  175.8 94.6 %copy-start.40 = (f32[4,512]{1,0:T(4,128)}, f32[4,512]{1,0:T(4,128)S(1)}, u32[]{:S(2)}) copy-start(f32[4,512]{1,0:T(4,128)S(1)} %log_add_fusion.2) | copy-start | bytes 24580
  204.8 76.6 %copy-start.38 = (f32[4,512]{1,0:T(4,128)}, f32[4,512]{1,0:T(4,128)S(1)}, u32[]{:S(2)}) copy-start(f32[4,512]{1,0:T(4,128)S(1)} %log_add_fusion.1) | copy-start | bytes 24580
  318.5 192.3 %all-gather.7.cloned.1.call-start = ((), (), s32[]{:S(2)}) async-start(), calls=%async_computation.6 | async-start | bytes 10485760 | tf_op jit(solution)/shard_map/all_gather | solution.py:127
  452.3 118.3 %all-gather.9.cloned.1.call-start = ((), (), s32[]{:S(2)}) async-start(), calls=%async_computation.8 | async-start | bytes 10485760 | tf_op jit(solution)/shard_map/all_gather | solution.py:142
  452.9 286.6 %reduce-scatter.9.cloned.1.call-start = ((), (), s32[]{:S(2)}) async-start(), calls=%async_computation.9 | async-start | bytes 20971520 | tf_op jit(solution)/shard_map/reduce_scatter | solution.py:148
  613.2 254.9 %reduce-scatter.7.cloned.1.call-start = ((), (), s32[]{:S(2)}) async-start(), calls=%async_computation.7 | async-start | bytes 20971520 | tf_op jit(solution)/shard_map/reduce_scatter | solution.py:133
  629.9 307.2 %all-gather.11.cloned.1.call-start = ((), (), s32[]{:S(2)}) async-start(), calls=%async_computation.10 | async-start | bytes 10485760 | tf_op jit(solution)/shard_map/all_gather | solution.py:157
  744.4 132.3 %copy-start.24 = (bf16[1024,1024]{1,0:T(8,128)(2,1)S(1)}, bf16[1024,1024]{1,0:T(8,128)(2,1)}, u32[]{:S(2)}) copy-start(bf16[1024,1024]{1,0:T(8,128)(2,1)} %param.71) | copy-start | bytes 6291460
  878.7 64.4 %copy-start.67 = (f32[4,512]{1,0:T(4,128)S(1)}, f32[4,512]{1,0:T(4,128)}, u32[]{:S(2)}) copy-start(f32[4,512]{1,0:T(4,128)} %copy-done.66) | copy-start | bytes 24580
  878.7 602.2 %reduce-scatter.11.cloned.1.call-start = ((), (), s32[]{:S(2)}) async-start(), calls=%async_computation.11 | async-start | bytes 20971520 | tf_op jit(solution)/shard_map/reduce_scatter | solution.py:208
  1354.6 536.7 %all-reduce.7.cloned.1.call-start = ((), (), s32[]{:S(2)}) async-start(), calls=%async_computation.12 | async-start | bytes 25165824 | tf_op jit(solution)/shard_map/psum | solution.py:216
  1404.7 76.2 %copy-start.14 = (bf16[1024,1024]{1,0:T(8,128)(2,1)S(1)}, bf16[1024,1024]{1,0:T(8,128)(2,1)}, u32[]{:S(2)}) copy-start(bf16[1024,1024]{1,0:T(8,128)(2,1)} %param.54) | copy-start | bytes 6291460
  1404.7 76.2 %copy-start.73 = (f32[1024]{0:T(1024)S(1)}, f32[1024]{0:T(1024)}, u32[]{:S(2)}) copy-start(f32[1024]{0:T(1024)} %copy-done.72) | copy-start | bytes 12292
  1404.7 76.2 %copy-start.75 = (f32[1024]{0:T(1024)S(1)}, f32[1024]{0:T(1024)}, u32[]{:S(2)}) copy-start(f32[1024]{0:T(1024)} %copy-done.74) | copy-start | bytes 12292
  1405.4 78.8 %copy-start.79 = (f32[1024]{0:T(1024)S(1)}, f32[1024]{0:T(1024)}, u32[]{:S(2)}) copy-start(f32[1024]{0:T(1024)} %copy-done.78) | copy-start | bytes 12292
  1405.4 78.9 %copy-start.77 = (f32[1024]{0:T(1024)S(1)}, f32[1024]{0:T(1024)}, u32[]{:S(2)}) copy-start(f32[1024]{0:T(1024)} %copy-done.76) | copy-start | bytes 12292
  (109 other events, 923.8 us)
Sparse Core Ops, SparseCore 0:
  16.7 60.9 all-gather.4
  318.6 126.0 reduce-scatter.4
  452.5 58.2 all-gather.6
  512.3 58.2 all-gather.8
  613.3 126.1 reduce-scatter.8
  741.9 126.1 reduce-scatter.6
  878.8 58.2 all-gather.10
  1354.7 126.0 reduce-scatter.10
  1487.4 403.8 all-reduce.6
where the time goes:
time: 1920 us; the launch traced here: 1910 us
  waiting for transfers between devices  943 us (49%)
  matrix products  579 us (30%)
  other arithmetic  253 us (13%)
  blocking collectives  67 us (3%)
  local copies, waits for them, and re-layouts  52.7 us (3%)
    psum x1, waiting for transfers between devices, shards(): lax.psum((joined_part[:, :head_cols], query_bias_part, joined_part[:, hea...  356 us
    reduce_scatter x1, waiting for transfers between devices, shards(): lax.psum_scatter(jnp.dot(mixed_heads, dense_weight, preferred_element_typ...  126 us
    reduce_scatter x1, waiting for transfers between devices, shards(): lax.psum_scatter(jnp.dot(active_low, down_weight, preferred_element_type=...  124 us
    reduce_scatter x1, waiting for transfers between devices, shards(): lax.psum_scatter(jnp.einsum('tf,df->td', hidden_grad, up_weight, preferre...  109 us
    convert_element_type x8, other arithmetic, shards(): score_grad = (prob_full * (prob_grad - row_dot)).astype(jnp.bfloat16)  107 us
    dot_general x8, matrix products, shards(): jnp.einsum('hqd,hkd->hqk', out_grad, value_block, preferred_element_type=...  102 us
    dot_general x8, matrix products, shards(): jnp.einsum('hqk,hqd->hkd', prob_low, out_grad, preferred_element_type=jnp...  80.3 us
    dot_general x8, matrix products, block_scores(): jnp.einsum('hqd,hkd->hqk', query_block, key_block, preferred_element_type...  78.1 us
  transfers between devices with their start and end apart: 9, of which 9 were waited for; matrix products, arithmetic and copies ran while one was open for 7% of the time, Pallas kernels for 0%

commit v1 on v0

--- a/solution.py
+++ b/solution.py
@@ -61,6 +61,23 @@
     down_bias,
     cotangent,
 ):
+
+    def see_racks(mesh_ax, axis_no, incoming_x):
+        chips = lax.axis_size(mesh_ax)
+        v1 = incoming_x
+        b_next = [(pp - 1, pp) for pp in range(1, chips)] + [(chips - 1, 0)]
+        j = 0
+        store = [v1]
+        while j < chips - 1:
+            v1 = lax.ppermute(v1, axis_name=mesh_ax, perm=b_next)
+            store += [v1]
+            j = j + 1
+        return jnp.roll(
+            jnp.concatenate([*reversed(store)], axis_no),
+            (lax.axis_index(mesh_ax) + 1) * v1.shape[axis_no],
+            axis_no,
+        )
+
     group_len = row_ids.shape[0]
     head_cols = query_weight.shape[1]
     head_count = head_cols // HD
@@ -124,7 +141,7 @@
         layer_norm, residual, post_gain.astype(jnp.float32), post_shift.astype(jnp.float32)
     )
     post_low = post_rows.astype(jnp.bfloat16)
-    post_all = lax.all_gather(post_low, "tensor", axis=0, tiled=True)
+    post_all = see_racks("tensor", 0, post_low)
     hidden = jnp.dot(post_all, up_weight, preferred_element_type=jnp.float32) + up_bias.astype(
         jnp.float32
     )

time: 1920 us -> 1930 us (level)
    ppermute x0 -> x3, waiting for transfers between devices: none -> 101 us  [see_racks(): v1 = lax.ppermute(v1, axis_name=mesh_ax, perm=b_next)]
    all_gather x1 -> x0, waiting for transfers between devices: 57.8 us -> none  [shards(): post_all = lax.all_gather(post_low, 'tensor', axis=0, tiled=True)]
    all_gather x1, waiting for transfers between devices: 43.8 us -> 0.02 us  [shards(): grad_all = lax.all_gather(cotangent, 'tensor', axis=0, tiled=True)]
    unnamed x246 -> x258, local copies, waits for them, and re-layouts: 44.4 us -> 61.5 us
  transfers between devices with their start and end apart: 9 -> 11, of which waited for: 9 -> 10; matrix products, arithmetic and copies ran while one was open for 7% -> 8% of each run, Pallas kernels for 0% -> 0%
where the time goes in v1:
time: 1930 us
  waiting for transfers between devices  941 us (49%)
  matrix products  578 us (30%)
  other arithmetic  256 us (13%)
  local copies, waits for them, and re-layouts  69.8 us (4%)
  blocking collectives  67 us (3%)
    psum x1, waiting for transfers between devices, shards(): lax.psum((joined_part[:, :head_cols], query_bias_part, joined_part[:, hea...  356 us
    reduce_scatter x1, waiting for transfers between devices, shards(): lax.psum_scatter(jnp.dot(mixed_heads, dense_weight, preferred_element_typ...  125 us
    reduce_scatter x1, waiting for transfers between devices, shards(): lax.psum_scatter(jnp.dot(active_low, down_weight, preferred_element_type=...  124 us
    reduce_scatter x1, waiting for transfers between devices, shards(): lax.psum_scatter(jnp.einsum('tf,df->td', hidden_grad, up_weight, preferre...  107 us
    convert_element_type x8, other arithmetic, shards(): score_grad = (prob_full * (prob_grad - row_dot)).astype(jnp.bfloat16)  107 us
    dot_general x8, matrix products, shards(): jnp.einsum('hqd,hkd->hqk', out_grad, value_block, preferred_element_type=...  101 us
    ppermute x3, waiting for transfers between devices, see_racks(): v1 = lax.ppermute(v1, axis_name=mesh_ax, perm=b_next)  101 us
    dot_general x8, matrix products, shards(): jnp.einsum('hqk,hqd->hkd', prob_low, out_grad, preferred_element_type=jnp...  80.3 us
  transfers between devices with their start and end apart: 11, of which 10 were waited for; matrix products, arithmetic and copies ran while one was open for 8% of the time, Pallas kernels for 0%

profile of v1, /device:TPU:0, one launch (start us, length us, event | category | flops | bytes accessed | tf_op | source)
XLA Modules:
  0.0 1928.7 jit_solution(2734707135812770526)
XLA Ops:
  60.1 17.6 all-gather.4.cloned.1.call-done
  204.9 18.2 fusion.236
  223.1 16.4 exponential_reduce_fusion
  319.3 125.5 %reduce-scatter.5.cloned.1.call-done = f32[1024,1024]{1,0:T(8,128)} async-done(((f32[4096,1024]{1,0:T(8,128)}), f32[1024,1024]{1,0:T(8,128)}) %reduce-scatter.5.cloned.1.call-update) | async-done | bytes 4194320 | tf_op jit(solution)/shard_map/reduce_scatter | solution.py:133
  450.7 61.6 %collective-permute-done = bf16[1024,1024]{1,0:T(8,128)(2,1)S(1)} collective-permute-done((bf16[1024,1024]{1,0:T(8,128)(2,1)S(1)}, bf16[1024,1024]{1,0:T(8,128)(2,1)S(1)}, u32[]{:S(2)}, u32[]{:S(2)}) %collective-permute-start) | collective-permute-done | bytes 2097184 | tf_op jit(solution)/shard_map/ppermute | solution.py:72
  513.6 30.1 %collective-permute-done.1 = bf16[1024,1024]{1,0:T(8,128)(2,1)} collective-permute-done((bf16[1024,1024]{1,0:T(8,128)(2,1)S(1)}, bf16[1024,1024]{1,0:T(8,128)(2,1)}, u32[]{:S(2)}, u32[]{:S(2)}) %collective-permute-start.1) | collective-permute-done | bytes 2097184 | tf_op jit(solution)/shard_map/ppermute | solution.py:72
  543.7 16.2 fusion.240
  589.1 26.7 %convert_reduce_fusion = (f32[1024]{0:T(1024)}, bf16[4096,1024]{1,0:T(8,128)(2,1)S(1)}, bf16[4096,1024]{1,0:T(8,128)(2,1)}) fusion(f32[4096,1024]{1,0:T(8,128)} %fusion.240, f32[1024]{0:T(1024)S(1)} %convert_element_type.310, bf16[1024,1024]{1,0:T(8,128)(2,1)S(1)} %copy-done, bf16[8192,1024]{1,0:T(8,128)(2,1)} %constant_dynamic-update-slice_fusion.3, ...), kind=kOutput, calls=%fused_computation.32 | convolution fusion | flops 8694791168 | bytes 44048388 | tf_op jit(solution)/shard_map/dot_general | solution.py:145
  632.7 16.8 fusion.239
  650.2 107.2 %reduce-scatter.9.cloned.1.call-done = f32[1024,1024]{1,0:T(8,128)} async-done(((f32[4096,1024]{1,0:T(8,128)}), f32[1024,1024]{1,0:T(8,128)}) %reduce-scatter.9.cloned.1.call-update) | async-done | bytes 4194320 | tf_op jit(solution)/shard_map/reduce_scatter | solution.py:165
  762.3 123.7 %reduce-scatter.7.cloned.1.call-done = f32[1024,1024]{1,0:T(8,128)} async-done(((f32[4096,1024]{1,0:T(8,128)}), f32[1024,1024]{1,0:T(8,128)}) %reduce-scatter.7.cloned.1.call-update) | async-done | bytes 4194320 | tf_op jit(solution)/shard_map/reduce_scatter | solution.py:150
  896.6 58.4 %all-gather.8.cloned.1.call-done = bf16[4096,1024]{1,0:T(8,128)(2,1)} async-done(((bf16[1024,1024]{1,0:T(8,128)(2,1)}), bf16[4096,1024]{1,0:T(8,128)(2,1)}) %all-gather.8.cloned.1.call-update) | async-done | bytes 8388624 | tf_op jit(solution)/shard_map/all_gather | solution.py:174
  1011.2 16.3 multiply_reduce_fusion.2
  1027.6 21.0 %multiply_reduce_fusion.1 = (f32[4,512]{1,0:T(4,128)}, f32[4,512,3584]{2,1,0:T(8,128)}) fusion(f32[4,512,3584]{2,1,0:T(8,128)} %get-tuple-element.284, f32[4,512]{1,0:T(4,128)S(1)} %copy-done.42, bf16[4,4096,64]{1,2,0:T(8,128)(2,1)S(1)} %bitcast.85, bf16[4,4096,64]{1,2,0:T(8,128)(2,1)} %bitcast.114), kind=kOutput, calls=%fused_computation.6 | convolution fusion | flops 961542144 | bytes 60833792 | tf_op jit(solution)/shard_map/hqd,hkd->hqk/dot_general | solution.py:205
  1048.6 22.6 %multiply_reduce_fusion = (f32[4,512]{1,0:T(4,128)}, f32[4,512,4096]{2,1,0:T(8,128)}) fusion(f32[4,512,4096]{2,1,0:T(8,128)} %get-tuple-element.286, f32[4,512]{1,0:T(4,128)S(1)} %copy-done.46, bf16[4,4096,64]{1,2,0:T(8,128)(2,1)S(1)} %bitcast.86, bf16[4,4096,64]{1,2,0:T(8,128)(2,1)S(1)} %bitcast.115), kind=kOutput, calls=%fused_computation.1 | convolution fusion | flops 1098905600 | bytes 69484544 | tf_op jit(solution)/shard_map/hqd,hkd->hqk/dot_general | solution.py:205
  1136.8 16.4 convert_reduce_fusion.3
  1235.8 16.8 multiply_convert_fusion.2
  1272.4 24.6 %multiply_convert_fusion.1 = bf16[4,512,3584]{2,1,0:T(8,128)(2,1)} fusion(f32[4,512,3584]{2,1,0:T(8,128)} %get-tuple-element.300, f32[4,512,3584]{2,1,0:T(8,128)} %get-tuple-element.284, f32[4,512]{1,0:T(4,128)S(1)} %copy-done.87, f32[4,512]{1,0:T(4,128)S(1)} %copy-done.42), kind=kLoop, calls=%fused_computation.5 | loop fusion | flops 29360128 | bytes 73416704 | tf_op jit(solution)/shard_map/convert_element_type | solution.py:209
  1313.7 27.6 %multiply_convert_fusion = bf16[4,512,4096]{2,1,0:T(8,128)(2,1)} fusion(f32[4,512,4096]{2,1,0:T(8,128)} %get-tuple-element.302, f32[4,512,4096]{2,1,0:T(8,128)} %get-tuple-element.286, f32[4,512]{1,0:T(4,128)S(1)} %copy-done.86, f32[4,512]{1,0:T(4,128)S(1)} %copy-done.46), kind=kLoop, calls=%fused_computation | loop fusion | flops 33554432 | bytes 83902464 | tf_op jit(solution)/shard_map/convert_element_type | solution.py:209
  1388.3 18.2 fusion.13
  1425.3 22.5 %all-reduce.3 = (f32[256]{0:T(256)}, f32[256]{0:T(256)}, f32[1024]{0:T(1024)}) all-reduce(f32[256]{0:T(256)S(1)} %reduce_sum.360, f32[256]{0:T(256)S(1)} %reduce_sum.362, f32[1024]{0:T(1024)S(1)} %copy-done.95), channel_id=1, replica_groups=mesh['dp'=8,'tensor'=4] {'dp'}, use_global_device_ids=true, to_apply=%region_42.43 | all-reduce | flops 1536 | bytes 12288 | tf_op jit(solution)/shard_map/psum | solution.py:233
  1447.7 51.1 %reduce-scatter.11.cloned.1.call-done = f32[1024,1024]{1,0:T(8,128)} async-done(((f32[4096,1024]{1,0:T(8,128)}), f32[1024,1024]{1,0:T(8,128)}) %reduce-scatter.11.cloned.1.call-update) | async-done | bytes 4194320 | tf_op jit(solution)/shard_map/reduce_scatter | solution.py:225
  1508.7 44.6 %all-reduce.2 = (f32[1024]{0:T(1024)}, f32[1024]{0:T(1024)}, f32[1024]{0:T(1024)}, f32[1024]{0:T(1024)}, f32[1024]{0:T(1024)}, /*index=5*/f32[1024]{0:T(1024)}) all-reduce(f32[1024]{0:T(1024)S(1)} %get-tuple-element.227, f32[1024]{0:T(1024)S(1)} %get-tuple-element.230, ...), channel_id=1, replica_groups=mesh['dp'=8,'tensor'=4] {'dp','tensor'}, use_global_device_ids=true, to_apply=%region_37.38 | all-reduce | flops 6144 | bytes 49152 | tf_op jit(solution)/shard_map/psum | solution.py:247
  1553.3 355.9 %all-reduce.7.cloned.1.call-done = (f32[1024,256]{1,0:T(8,128)}, f32[1024,256]{1,0:T(8,128)}, f32[1024,256]{1,0:T(8,128)}, f32[256,1024]{1,0:T(8,128)}, f32[1024,1024]{1,0:T(8,128)}, /*index=5*/f32[1024,1024]{1,0:T(8,128)}) async-done(((f32[1024,256]{1,0:T(8,128)}, f32[1024,256]{1,0:T(8,128)}, f32[1024,256]{1,0:T(8,128)}, f32[256,1024]{1,0:T(8,128)}, f32[1024,1024]{1,0:T(8,128)}, ...) | async-done | bytes 12582928 | tf_op jit(solution)/shard_map/psum | solution.py:233
  (439 shorter events, 657.2 us)
Async XLA Ops:
  7.2 581.9 %copy-start = (bf16[1024,1024]{1,0:T(8,128)(2,1)S(1)}, bf16[1024,1024]{1,0:T(8,128)(2,1)}, u32[]{:S(2)}) copy-start(bf16[1024,1024]{1,0:T(8,128)(2,1)} %param.67) | copy-start | bytes 6291460
  7.2 70.5 %all-gather.4.cloned.1.call-start = ((), (), s32[]{:S(2)}) async-start(), calls=%async_computation.4 | async-start | bytes 10485760 | tf_op jit(solution)/shard_map/all_gather | solution.py:97
  16.6 428.2 %reduce-scatter.5.cloned.1.call-start = ((), (), s32[]{:S(2)}) async-start(), calls=%async_computation.5 | async-start | bytes 20971520 | tf_op jit(solution)/shard_map/reduce_scatter | solution.py:133
  94.4 145.1 %copy-start.69 = (f32[4,512]{1,0:T(4,128)}, f32[4,512]{1,0:T(4,128)S(1)}, u32[]{:S(2)}) copy-start(f32[4,512]{1,0:T(4,128)S(1)} %log_add_fusion.7) | copy-start | bytes 24580
  102.0 139.0 %copy-start.66 = (f32[4,512]{1,0:T(4,128)}, f32[4,512]{1,0:T(4,128)S(1)}, u32[]{:S(2)}) copy-start(f32[4,512]{1,0:T(4,128)S(1)} %log_add_fusion.6) | copy-start | bytes 24580
  110.3 133.1 %copy-start.62 = (f32[4,512]{1,0:T(4,128)}, f32[4,512]{1,0:T(4,128)S(1)}, u32[]{:S(2)}) copy-start(f32[4,512]{1,0:T(4,128)S(1)} %log_add_fusion.5) | copy-start | bytes 24580
  128.6 122.2 %copy-start.71 = (f32[4,512]{1,0:T(4,128)}, f32[4,512]{1,0:T(4,128)S(1)}, u32[]{:S(2)}) copy-start(f32[4,512]{1,0:T(4,128)S(1)} %log_add_fusion.4) | copy-start | bytes 24580
  151.3 109.0 %copy-start.54 = (f32[4,512]{1,0:T(4,128)}, f32[4,512]{1,0:T(4,128)S(1)}, u32[]{:S(2)}) copy-start(f32[4,512]{1,0:T(4,128)S(1)} %log_add_fusion.3) | copy-start | bytes 24580
  175.9 94.5 %copy-start.43 = (f32[4,512]{1,0:T(4,128)}, f32[4,512]{1,0:T(4,128)S(1)}, u32[]{:S(2)}) copy-start(f32[4,512]{1,0:T(4,128)S(1)} %log_add_fusion.2) | copy-start | bytes 24580
  204.9 76.5 %copy-start.41 = (f32[4,512]{1,0:T(4,128)}, f32[4,512]{1,0:T(4,128)S(1)}, u32[]{:S(2)}) copy-start(f32[4,512]{1,0:T(4,128)S(1)} %log_add_fusion.1) | copy-start | bytes 24580
  318.5 225.2 %all-gather.6.cloned.1.call-start = ((), (), s32[]{:S(2)}) async-start(), calls=%async_computation.7 | async-start | bytes 10485760 | tf_op jit(solution)/shard_map/all_gather | solution.py:159
  319.2 438.2 %reduce-scatter.9.cloned.1.call-start = ((), (), s32[]{:S(2)}) async-start(), calls=%async_computation.8 | async-start | bytes 20971520 | tf_op jit(solution)/shard_map/reduce_scatter | solution.py:165
  448.9 94.8 %copy-start.99 = (bf16[1024]{0:T(1024)(128)(2,1)S(1)}, bf16[1024]{0:T(1024)(128)(2,1)}, u32[]{:S(2)}) copy-start(bf16[1024]{0:T(1024)(128)(2,1)} %param.68) | copy-start | bytes 6148
  450.3 62.0 %collective-permute-start = (bf16[1024,1024]{1,0:T(8,128)(2,1)S(1)}, bf16[1024,1024]{1,0:T(8,128)(2,1)S(1)}, u32[]{:S(2)}, u32[]{:S(2)}) collective-permute-start(bf16[1024,1024]{1,0:T(8,128)(2,1)S(1)} %add_convert_fusion.1), channel_id=1, source_target_pairs={{0,1},{1,2},{2,3},{3,0},{4,5},{5,6},{6,7},{7,4},{8,9},{9,10},{10,1... | collective-permute-start | bytes 6291464 | tf_op jit(solution)/shard_map/ppermute | solution.py:72
  513.6 30.1 %collective-permute-start.1 = (bf16[1024,1024]{1,0:T(8,128)(2,1)S(1)}, bf16[1024,1024]{1,0:T(8,128)(2,1)}, u32[]{:S(2)}, u32[]{:S(2)}) collective-permute-start(bf16[1024,1024]{1,0:T(8,128)(2,1)S(1)} %collective-permute-done), channel_id=1, source_target_pairs={{0,1},{1,2},{2,3},{3,0},{4,5},{5,6},{6,7},{7,4},{8,9},{9,10},{10,1... | collective-permute-start | bytes 6291464 | tf_op jit(solution)/shard_map/ppermute | solution.py:72
  543.7 25.8 %collective-permute-start.2 = (bf16[1024,1024]{1,0:T(8,128)(2,1)}, bf16[1024,1024]{1,0:T(8,128)(2,1)}, u32[]{:S(2)}, u32[]{:S(2)}) collective-permute-start(bf16[1024,1024]{1,0:T(8,128)(2,1)} %collective-permute-done.1), channel_id=1, source_target_pairs={{0,1},{1,2},{2,3},{3,0},{4,5},{5,6},{6,7},{7,4},{8,9},{9,10},{10,1... | collective-permute-start | bytes 6291464 | tf_op jit(solution)/shard_map/ppermute | solution.py:72
  631.1 254.9 %reduce-scatter.7.cloned.1.call-start = ((), (), s32[]{:S(2)}) async-start(), calls=%async_computation.6 | async-start | bytes 20971520 | tf_op jit(solution)/shard_map/reduce_scatter | solution.py:150
  649.6 305.5 %all-gather.8.cloned.1.call-start = ((), (), s32[]{:S(2)}) async-start(), calls=%async_computation.9 | async-start | bytes 10485760 | tf_op jit(solution)/shard_map/all_gather | solution.py:174
  762.3 132.3 %copy-start.25 = (bf16[1024,1024]{1,0:T(8,128)(2,1)S(1)}, bf16[1024,1024]{1,0:T(8,128)(2,1)}, u32[]{:S(2)}) copy-start(bf16[1024,1024]{1,0:T(8,128)(2,1)} %param.71) | copy-start | bytes 6291460
  896.6 602.2 %reduce-scatter.11.cloned.1.call-start = ((), (), s32[]{:S(2)}) async-start(), calls=%async_computation.10 | async-start | bytes 20971520 | tf_op jit(solution)/shard_map/reduce_scatter | solution.py:225
  1372.5 536.7 %all-reduce.7.cloned.1.call-start = ((), (), s32[]{:S(2)}) async-start(), calls=%async_computation.11 | async-start | bytes 25165824 | tf_op jit(solution)/shard_map/psum | solution.py:233
  1422.5 76.3 %copy-start.76 = (f32[1024]{0:T(1024)S(1)}, f32[1024]{0:T(1024)}, u32[]{:S(2)}) copy-start(f32[1024]{0:T(1024)} %copy-done.75) | copy-start | bytes 12292
  1423.2 79.0 %copy-start.82 = (f32[1024]{0:T(1024)S(1)}, f32[1024]{0:T(1024)}, u32[]{:S(2)}) copy-start(f32[1024]{0:T(1024)} %copy-done.81) | copy-start | bytes 12292
  1423.2 79.0 %copy-start.80 = (f32[1024]{0:T(1024)S(1)}, f32[1024]{0:T(1024)}, u32[]{:S(2)}) copy-start(f32[1024]{0:T(1024)} %copy-done.79) | copy-start | bytes 12292
  (114 other events, 1131.5 us)
Sparse Core Ops, SparseCore 0:
  16.7 60.9 all-gather.3
  318.6 126.1 reduce-scatter.4
  446.4 78.6 all-gather.5
  631.3 126.1 reduce-scatter.8
  759.9 126.1 reduce-scatter.6
  896.7 58.2 all-gather.7
  1372.6 126.1 reduce-scatter.10
  1505.4 403.8 all-reduce.6
